TPU v7x, 256 devices: a whole 4x4x8 slice. The times are simulated.
256 devices in a mesh: dp: 32 (over z_hi, y, x), tensor: 8 (over z_lo, core).
Axes of the slice: x: 4, y: 4, z: 8 (z_hi: 2, z_lo: 4; z = z_hi * 4 + z_lo), core: 2. Of those that a mesh axis runs over, the one named last changes fastest.
Arguments:
- queries: bfloat16 [32768, 3072], P('dp', 'tensor'), may hold values from -70 to 70
- keys: bfloat16 [32768, 3072], P('dp', 'tensor'), may hold values from -5 to 5
- values: bfloat16 [32768, 3072], P('dp', 'tensor'), may hold values from -6 to 6
- out_gradient: bfloat16 [32768, 5120], P(('dp', 'tensor')), may hold values from -24 to 24
- out_weight: bfloat16 [3072, 5120], P('tensor'), may hold values from -0.109375 to 0.109375
- segments: int32 [32, 8], replicated, may hold values from 0 to 7, as said below
- counts: int32 [32], replicated, may hold values from 1 to 4, as said below
Outputs:
- query_gradient: bfloat16 [32768, 3072], P('dp', 'tensor')
- key_gradient: bfloat16 [32768, 3072], P('dp', 'tensor')
- value_gradient: bfloat16 [32768, 3072], P('dp', 'tensor')
- weight_gradient: float32 [5120, 3072], P('dp', 'tensor')
Inputs may be any that keep to these rules, and one draw needn't show every extreme that they name: `segments`: along each row ids never fall; each protein spans 1 to 4 consecutive blocks, and some protein spans exactly 4; the last counts[r] blocks of replica r are whole proteins. counts[r] equals counts[(r + 16) mod 32].
All inputs are finite; a program needn't handle non-finite values.
Results may differ from a plain program's by a relative error of at most 0.025.
Values may be sent and summed in bfloat16 or wider, within the bound.
No kernel may reach another device: no remote copies, remote signals or barrier semaphores. Data moves between devices by JAX's collectives and lax.ppermute only.
A program may use at most 128 MiB of HBM per device.

v0:
```python
import jax
import jax.numpy as jnp
from jax import lax
from jax.sharding import Mesh
from jax.sharding import PartitionSpec as P

HEAD_SIZE = 128
BLOCK = 128
DP = ("dp_0", "dp_1", "dp_2")
DP_TENSOR = ("dp_0", "dp_1", "dp_2", "tensor")
masked_score = -1e30


def swapped(x, axis, distance):
    return lax.ppermute(x, axis, [(i, i ^ 1 << distance) for i in range(lax.axis_size(axis))])


def reduced_to_own(tiles, axes, order):
    shape = [lax.axis_size(a) for a in axes]
    tiles = tiles.reshape(*shape, *tiles.shape[1:])
    tiles = tiles.transpose(*order, *range(len(axes), tiles.ndim))
    tiles = tiles.reshape(-1, *tiles.shape[len(axes) :])
    for k in order:
        tiles = lax.psum_scatter(tiles, axes[k], scatter_dimension=0, tiled=True)
    return tiles[0]


def cut_along(x, dim, devices):
    shape = x.shape
    tiles = x.reshape(*shape[:dim], devices, shape[dim] // devices, *shape[dim + 1 :])
    return jnp.moveaxis(tiles, dim, 0)


def summed_rows_2(x, axes, order, dim):
    devices = lax.axis_size(axes)
    return reduced_to_own(cut_along(x, dim, devices), axes, order)


def attend(query, key_rows, value, gradient, block_ids):
    length, inner = query.shape
    heads = inner // HEAD_SIZE
    scale = HEAD_SIZE ** (-0.5)
    total_blocks = block_ids.shape[0]
    window = total_blocks // 2

    def split(array, rows):
        return array.reshape(rows, heads, HEAD_SIZE)

    def visit(carry, index):
        key_total, value_total = carry
        own = block_ids[index]
        first = jnp.argmax(block_ids == own)
        start = jnp.minimum(first, total_blocks - window)
        query_block = split(lax.dynamic_slice_in_dim(query, index * BLOCK, BLOCK, 0), BLOCK)
        grad_block = split(lax.dynamic_slice_in_dim(gradient, index * BLOCK, BLOCK, 0), BLOCK)
        window_ids = lax.dynamic_slice_in_dim(block_ids, start, window, 0)
        key_window = split(
            lax.dynamic_slice_in_dim(key_rows, start * BLOCK, window * BLOCK, 0), window * BLOCK
        )
        value_window = split(
            lax.dynamic_slice_in_dim(value, start * BLOCK, window * BLOCK, 0), window * BLOCK
        )
        score_tiles = []
        grad_tiles = []
        for tile in range(window):
            key_tile = key_window[tile * BLOCK : (tile + 1) * BLOCK]
            value_tile = value_window[tile * BLOCK : (tile + 1) * BLOCK]

            def near(key_tile=key_tile, value_tile=value_tile):
                return (
                    jnp.einsum(
                        "qhd,khd->hqk", query_block, key_tile, preferred_element_type=jnp.float32
                    )
                    * scale,
                    jnp.einsum(
                        "qhd,khd->hqk", grad_block, value_tile, preferred_element_type=jnp.float32
                    ),
                )

            def far():
                return (
                    jnp.full((heads, BLOCK, BLOCK), masked_score, jnp.float32),
                    jnp.zeros((heads, BLOCK, BLOCK), jnp.float32),
                )

            score_tile, grad_tile = lax.cond(window_ids[tile] == own, near, far)
            score_tiles.append(score_tile)
            grad_tiles.append(grad_tile)
        scores = jnp.concatenate(score_tiles, axis=2)
        chance_gradient = jnp.concatenate(grad_tiles, axis=2)
        highest = jnp.max(scores, axis=2, keepdims=True)
        weights = jnp.exp(scores - highest)
        chances = weights / jnp.sum(weights, axis=2, keepdims=True)
        chance_weights = chances.astype(jnp.bfloat16)
        output_sum = jnp.zeros((BLOCK, heads, HEAD_SIZE), jnp.float32)
        for tile in range(window):
            value_tile = value_window[tile * BLOCK : (tile + 1) * BLOCK]
            weight_tile = chance_weights[:, :, tile * BLOCK : (tile + 1) * BLOCK]
            output_sum = output_sum + lax.cond(
                window_ids[tile] == own,
                lambda weight_tile=weight_tile, value_tile=value_tile: jnp.einsum(
                    "hqk,khd->qhd", weight_tile, value_tile, preferred_element_type=jnp.float32
                ),
                lambda: jnp.zeros((BLOCK, heads, HEAD_SIZE), jnp.float32),
            )
        head_output = output_sum.astype(jnp.bfloat16)
        centering = jnp.sum(
            grad_block.astype(jnp.float32) * head_output.astype(jnp.float32), axis=2
        )
        score_gradient = (
            chances * (chance_gradient - jnp.transpose(centering)[:, :, None])
        ).astype(jnp.bfloat16)
        query_sum = jnp.zeros((BLOCK, heads, HEAD_SIZE), jnp.float32)
        key_pieces = []
        value_pieces = []
        for tile in range(window):
            key_tile = key_window[tile * BLOCK : (tile + 1) * BLOCK]
            slope_tile = score_gradient[:, :, tile * BLOCK : (tile + 1) * BLOCK]
            weight_tile = chance_weights[:, :, tile * BLOCK : (tile + 1) * BLOCK]

            def near_back(key_tile=key_tile, slope_tile=slope_tile, weight_tile=weight_tile):
                return (
                    jnp.einsum(
                        "hqk,khd->qhd", slope_tile, key_tile, preferred_element_type=jnp.float32
                    ),
                    jnp.einsum(
                        "hqk,qhd->khd", slope_tile, query_block, preferred_element_type=jnp.float32
                    ),
                    jnp.einsum(
                        "hqk,qhd->khd", weight_tile, grad_block, preferred_element_type=jnp.float32
                    ),
                )

            def far_back():
                empty = jnp.zeros((BLOCK, heads, HEAD_SIZE), jnp.float32)
                return (empty, empty, empty)

            query_part, key_part, value_part = lax.cond(
                window_ids[tile] == own, near_back, far_back
            )
            query_sum = query_sum + query_part
            key_pieces.append(key_part.reshape(BLOCK, inner))
            value_pieces.append(value_part.reshape(BLOCK, inner))
        key_window_sum = jnp.concatenate(key_pieces, axis=0)
        value_window_sum = jnp.concatenate(value_pieces, axis=0)
        key_total = lax.dynamic_update_slice_in_dim(
            key_total,
            lax.dynamic_slice_in_dim(key_total, start * BLOCK, window * BLOCK, 0) + key_window_sum,
            start * BLOCK,
            0,
        )
        value_total = lax.dynamic_update_slice_in_dim(
            value_total,
            lax.dynamic_slice_in_dim(value_total, start * BLOCK, window * BLOCK, 0)
            + value_window_sum,
            start * BLOCK,
            0,
        )
        query_block_grad = (query_sum * scale).astype(jnp.bfloat16).reshape(BLOCK, inner)
        return ((key_total, value_total), (query_block_grad, head_output.reshape(BLOCK, inner)))

    start_totals = (
        jnp.zeros((length, inner), jnp.float32),
        jnp.zeros((length, inner), jnp.float32),
    )
    totals, stacked = lax.scan(visit, start_totals, jnp.arange(total_blocks, dtype=jnp.int32))
    query_local = stacked[0].reshape(length, inner)
    head_output = stacked[1].reshape(length, inner)
    key_local = (totals[0] * scale).astype(jnp.bfloat16)
    value_local = totals[1].astype(jnp.bfloat16)
    return (query_local, key_local, value_local, head_output)


def shards(queries, keys, values, out_gradient, out_weight, segments, counts):
    full_gradient = lax.all_gather(out_gradient, "tensor", axis=0, tiled=True)
    head_gradient = lax.dot_general(
        full_gradient, out_weight, (((1,), (1,)), ((), ())), preferred_element_type=jnp.float32
    ).astype(jnp.bfloat16)
    replicas = lax.axis_size(DP)
    halfway = replicas // 2
    position = lax.axis_index(DP)
    blocks = segments.shape[1]
    block_rows = queries.shape[0] // blocks
    trailing = blocks // 2 * block_rows
    moving = lax.dynamic_index_in_dim(counts, position, 0, keepdims=False)
    own_blocks = lax.dynamic_index_in_dim(segments, position, 0, keepdims=False)
    block_moved = jnp.arange(blocks, dtype=jnp.int32) >= blocks - moving
    row_moved = jnp.repeat(block_moved, block_rows)[-trailing:, None]
    flip_bit = halfway.bit_length() - 1

    def settle(local, arrived):
        upper = jnp.where(row_moved, arrived, local[-trailing:])
        return jnp.concatenate([local[:-trailing], upper], axis=0)

    query_local, key_local, value_local, head_output = attend(
        queries, keys, values, head_gradient, own_blocks
    )
    arrived = swapped(
        (query_local[-trailing:], key_local[-trailing:], value_local[-trailing:]), DP, flip_bit
    )
    query_gradient = settle(query_local, arrived[0])
    key_gradient = settle(key_local, arrived[1])
    value_gradient = settle(value_local, arrived[2])
    weight_gradient = summed_rows_2(
        lax.dot_general(
            full_gradient, head_output, (((0,), (0,)), ((), ())), preferred_element_type=jnp.float32
        )
        / replicas,
        DP,
        (1, 2, 0),
        0,
    )
    return (query_gradient, key_gradient, value_gradient, weight_gradient)


def solution(mesh):
    split = Mesh(
        mesh.devices.reshape(2, 4, 4, mesh.shape["tensor"]), ("dp_0", "dp_1", "dp_2", "tensor")
    )
    placed = (
        P(DP, "tensor"),
        P(DP, "tensor"),
        P(DP, "tensor"),
        P(DP_TENSOR, None),
        P("tensor", None),
        P(),
        P(),
    )
    return jax.shard_map(
        shards,
        mesh=split,
        in_specs=placed,
        out_specs=(P(DP, "tensor"), P(DP, "tensor"), P(DP, "tensor"), P(DP, "tensor")),
        check_vma=False,
    )
```

profile of v0, /device:TPU:1, one launch (start us, length us, event | category | flops | bytes accessed | tf_op | source)
XLA Modules:
  0.0 550.3 jit_solution(16349101674922859828)
XLA Ops:
  8.2 116.8 %all-gather.2.cloned.1.call-done = bf16[1024,5120]{1,0:T(8,128)(2,1)} async-done(((bf16[128,5120]{1,0:T(8,128)(2,1)}), bf16[1024,5120]{1,0:T(8,128)(2,1)}) %all-gather.2.cloned.1.call-update) | async-done | bytes 10485776 | tf_op jit(solution)/shard_map/all_gather | solution.py:175
  125.0 9.5 %convolution_convert_fusion = bf16[1024,384]{1,0:T(8,128)(2,1)S(1)} fusion(bf16[1024,5120]{1,0:T(8,128)(2,1)} %all-gather.2.cloned.1.call-done, bf16[384,5120]{1,0:T(8,128)(2,1)} %param.37), kind=kOutput, calls=%fused_computation.57 | convolution fusion | flops 4026925056 | bytes 15204352 | tf_op jit(solution)/shard_map/dot_general | solution.py:176
  134.5 1.2 broadcast.83.clone
  135.8 1.3 broadcast.83.clone2
  137.0 223.8 %while.16 = (s32[]{:T(128)}, f32[1024,384]{1,0:T(8,128)}, f32[1024,384]{1,0:T(8,128)}, bf16[8,128,384]{1,2,0:T(8,128)(2,1)}, bf16[8,128,384]{2,1,0:T(8,128)(2,1)...) while((s32[]{:T(128)}, f32[1024,384]{1,0:T(8,128)}, ...), condition=%wide.region_32.33_spmd, body=%wide.region_0.32_spmd.sunk | while | flops 308919232 | bytes 47705920 | solution.py:166
  140.3 1.3 compare_reduce_fusion.2
  142.2 1.3 constant_dynamic-slice_fusion.17
  157.0 1.5 constant_dynamic-slice_fusion.15
  158.8 1.0 maximum_add_fusion.5
  160.1 0.9 constant_dynamic-update-slice_fusion.9
  161.7 0.9 constant_dynamic-update-slice_fusion.8
  166.7 1.3 compare_reduce_fusion.2
  168.7 1.3 constant_dynamic-slice_fusion.17
  183.4 1.5 constant_dynamic-slice_fusion.15
  185.2 1.0 maximum_add_fusion.5
  186.5 0.9 constant_dynamic-update-slice_fusion.9
  188.1 1.0 constant_dynamic-update-slice_fusion.8
  193.1 1.3 compare_reduce_fusion.2
  195.1 1.3 constant_dynamic-slice_fusion.17
  209.8 1.5 constant_dynamic-slice_fusion.15
  211.6 1.0 maximum_add_fusion.5
  214.5 0.9 constant_dynamic-update-slice_fusion.8
  219.5 1.3 compare_reduce_fusion.2
  221.5 1.3 constant_dynamic-slice_fusion.17
  236.2 1.5 constant_dynamic-slice_fusion.15
  238.0 1.0 maximum_add_fusion.5
  239.3 0.9 constant_dynamic-update-slice_fusion.9
  240.9 0.9 constant_dynamic-update-slice_fusion.8
  245.9 1.3 compare_reduce_fusion.2
  247.9 1.3 constant_dynamic-slice_fusion.17
  265.8 1.5 constant_dynamic-slice_fusion.15
  267.6 1.0 maximum_add_fusion.5
  268.9 0.9 constant_dynamic-update-slice_fusion.9
  270.5 0.9 constant_dynamic-update-slice_fusion.8
  275.5 1.3 compare_reduce_fusion.2
  277.4 1.3 constant_dynamic-slice_fusion.17
  295.3 1.5 constant_dynamic-slice_fusion.15
  297.1 1.0 maximum_add_fusion.5
  298.4 0.9 constant_dynamic-update-slice_fusion.9
  300.1 0.9 constant_dynamic-update-slice_fusion.8
  305.0 1.3 compare_reduce_fusion.2
  307.0 1.3 constant_dynamic-slice_fusion.17
  324.9 1.5 constant_dynamic-slice_fusion.15
  326.7 1.0 maximum_add_fusion.5
  328.0 0.9 constant_dynamic-update-slice_fusion.9
  334.6 1.3 compare_reduce_fusion.2
  336.5 1.3 constant_dynamic-slice_fusion.17
  354.4 1.5 constant_dynamic-slice_fusion.15
  356.2 1.0 maximum_add_fusion.5
  357.5 0.9 constant_dynamic-update-slice_fusion.9
  360.9 11.7 %multiply_bitcast_fusion = f32[5120,384]{0,1:T(8,128)} fusion(bf16[1024,384]{1,0:T(8,128)(2,1)} %bitcast.202, bf16[1024,5120]{1,0:T(8,128)(2,1)} %all-gather.2.cloned.1.call-done), kind=kOutput, calls=%fused_computation.55 | convolution fusion | flops 4028497920 | bytes 19136512 | tf_op jit(solution)/shard_map/dot_general | solution.py:205
  372.6 9.1 %copy.87 = f32[5120,384]{1,0:T(8,128)} copy(f32[5120,384]{0,1:T(8,128)} %multiply_bitcast_fusion) | data formatting | bytes 15728640 | tf_op jit(solution)/shard_map/div | solution.py:205
  381.7 7.1 %copy.88 = f32[4,4,2,160,384]{4,3,2,1,0:T(8,128)} copy(f32[4,4,2,160,384]{4,3,1,0,2:T(8,128)} %bitcast.173) | data formatting | bytes 15728640 | tf_op jit(solution)/shard_map/transpose | solution.py:21
  388.9 82.4 %reduce-scatter.4.cloned.1.call-done = f32[8,160,384]{2,1,0:T(8,128)} async-done(((f32[32,160,384]{2,1,0:T(8,128)}), f32[8,160,384]{2,1,0:T(8,128)}) %reduce-scatter.4.cloned.1.call-update) | async-done | bytes 1966096 | tf_op jit(solution)/shard_map/reduce_scatter | solution.py:24
  471.7 5.5 %collective-permute-start = (bf16[512,384]{1,0:T(8,128)(2,1)S(1)}, bf16[512,384]{1,0:T(8,128)(2,1)}, u32[]{:S(2)}, u32[]{:S(2)}) collective-permute-start(bf16[512,384]{1,0:T(8,128)(2,1)S(1)} %bitcast.201), channel_id=1, source_target_pairs={{0,128},{8,136},{16,144},{24,152},{32,160},{40,168},{48,176},{56,1... | collective-permute-start | bytes 1179656 | tf_op jit(solution)/shard_map/ppermute | solution.py:15
  477.2 1.7 multiply_convert_fusion.1
  479.3 5.4 collective-permute-start.2
  485.9 19.0 %reduce-scatter.6.cloned.1.call-done = f32[2,160,384]{2,1,0:T(8,128)} async-done(((f32[8,160,384]{2,1,0:T(8,128)}), f32[2,160,384]{2,1,0:T(8,128)}) %reduce-scatter.6.cloned.1.call-update) | async-done | bytes 491536 | tf_op jit(solution)/shard_map/reduce_scatter | solution.py:24
  505.3 11.7 %collective-permute-done.2 = bf16[512,384]{1,0:T(8,128)(2,1)} collective-permute-done((bf16[512,384]{1,0:T(8,128)(2,1)S(1)}, bf16[512,384]{1,0:T(8,128)(2,1)}, u32[]{:S(2)}, u32[]{:S(2)}) %collective-permute-start.2) | collective-permute-done | bytes 393248 | tf_op jit(solution)/shard_map/ppermute | solution.py:15
  517.0 1.5 fusion.19
  518.5 1.0 pad_maximum_fusion.2
  519.5 1.0 pad_maximum_fusion.1
  520.5 1.0 pad_maximum_fusion
  521.4 22.3 %reduce-scatter.8.cloned.1.call-done = f32[1,160,384]{2,1,0:T(8,128)} async-done(((f32[2,160,384]{2,1,0:T(8,128)}), f32[1,160,384]{2,1,0:T(8,128)}) %reduce-scatter.8.cloned.1.call-update) | async-done | bytes 245776 | tf_op jit(solution)/shard_map/reduce_scatter | solution.py:24
  (694 shorter events, 128.5 us)
Async XLA Ops:
  7.2 0.8 copy-start
  7.2 117.9 %all-gather.2.cloned.1.call-start = ((), (), s32[]{:S(2)}) async-start(), calls=%async_computation.3 | async-start | bytes 11796480 | tf_op jit(solution)/shard_map/all_gather | solution.py:175
  7.9 463.4 %reduce-scatter.4.cloned.1.call-start = ((), (), s32[]{:S(2)}) async-start(), calls=%async_computation.4 | async-start | bytes 9830400 | tf_op jit(solution)/shard_map/reduce_scatter | solution.py:24
  137.0 10.6 %copy-start.8 = (bf16[1024,384]{1,0:T(8,128)(2,1)}, bf16[1024,384]{1,0:T(8,128)(2,1)S(1)}, u32[]{:S(2)}) copy-start(bf16[1024,384]{1,0:T(8,128)(2,1)S(1)} %get-tuple-element.628) | copy-start | bytes 2359300 | tf_op jit(solution)/shard_map/while
  156.2 2.2 copy-start.3
  156.3 2.2 copy-start.5
  160.1 1.2 copy-start.4
  161.4 1.2 copy-start.6
  161.4 2.0 copy-start.9
  163.5 10.6 %copy-start.8 = (bf16[1024,384]{1,0:T(8,128)(2,1)}, bf16[1024,384]{1,0:T(8,128)(2,1)S(1)}, u32[]{:S(2)}) copy-start(bf16[1024,384]{1,0:T(8,128)(2,1)S(1)} %get-tuple-element.628) | copy-start | bytes 2359300 | tf_op jit(solution)/shard_map/while
  182.7 2.2 copy-start.3
  182.7 2.2 copy-start.5
  186.5 1.2 copy-start.4
  187.8 1.3 copy-start.6
  187.8 2.0 copy-start.9
  189.9 10.6 %copy-start.8 = (bf16[1024,384]{1,0:T(8,128)(2,1)}, bf16[1024,384]{1,0:T(8,128)(2,1)S(1)}, u32[]{:S(2)}) copy-start(bf16[1024,384]{1,0:T(8,128)(2,1)S(1)} %get-tuple-element.628) | copy-start | bytes 2359300 | tf_op jit(solution)/shard_map/while
  209.1 2.2 copy-start.3
  209.1 2.2 copy-start.5
  212.9 1.2 copy-start.4
  214.2 1.2 copy-start.6
  214.3 2.0 copy-start.9
  216.3 10.6 %copy-start.8 = (bf16[1024,384]{1,0:T(8,128)(2,1)}, bf16[1024,384]{1,0:T(8,128)(2,1)S(1)}, u32[]{:S(2)}) copy-start(bf16[1024,384]{1,0:T(8,128)(2,1)S(1)} %get-tuple-element.628) | copy-start | bytes 2359300 | tf_op jit(solution)/shard_map/while
  235.5 2.2 copy-start.3
  235.5 2.2 copy-start.5
  239.3 1.2 copy-start.4
  240.6 1.2 copy-start.6
  240.7 2.0 copy-start.9
  242.7 10.6 %copy-start.8 = (bf16[1024,384]{1,0:T(8,128)(2,1)}, bf16[1024,384]{1,0:T(8,128)(2,1)S(1)}, u32[]{:S(2)}) copy-start(bf16[1024,384]{1,0:T(8,128)(2,1)S(1)} %get-tuple-element.628) | copy-start | bytes 2359300 | tf_op jit(solution)/shard_map/while
  265.0 2.2 copy-start.3
  265.0 2.2 copy-start.5
  268.9 1.2 copy-start.4
  270.2 1.2 copy-start.6
  270.2 2.0 copy-start.9
  272.2 10.6 %copy-start.8 = (bf16[1024,384]{1,0:T(8,128)(2,1)}, bf16[1024,384]{1,0:T(8,128)(2,1)S(1)}, u32[]{:S(2)}) copy-start(bf16[1024,384]{1,0:T(8,128)(2,1)S(1)} %get-tuple-element.628) | copy-start | bytes 2359300 | tf_op jit(solution)/shard_map/while
  294.6 2.2 copy-start.3
  294.6 2.2 copy-start.5
  298.4 1.2 copy-start.4
  299.8 1.2 copy-start.6
  299.8 2.0 copy-start.9
  301.8 10.6 %copy-start.8 = (bf16[1024,384]{1,0:T(8,128)(2,1)}, bf16[1024,384]{1,0:T(8,128)(2,1)S(1)}, u32[]{:S(2)}) copy-start(bf16[1024,384]{1,0:T(8,128)(2,1)S(1)} %get-tuple-element.628) | copy-start | bytes 2359300 | tf_op jit(solution)/shard_map/while
  324.1 2.2 copy-start.3
  324.1 2.2 copy-start.5
  328.0 1.2 copy-start.4
  329.3 1.2 copy-start.6
  329.3 2.0 copy-start.9
  331.3 10.6 %copy-start.8 = (bf16[1024,384]{1,0:T(8,128)(2,1)}, bf16[1024,384]{1,0:T(8,128)(2,1)S(1)}, u32[]{:S(2)}) copy-start(bf16[1024,384]{1,0:T(8,128)(2,1)S(1)} %get-tuple-element.628) | copy-start | bytes 2359300 | tf_op jit(solution)/shard_map/while
  353.7 2.2 copy-start.3
  353.7 2.2 copy-start.5
  357.5 1.2 copy-start.4
  358.9 1.2 copy-start.6
  358.9 2.0 copy-start.9
  388.8 82.6 %copy-start.7 = (bf16[8,128,384]{1,2,0:T(8,128)(2,1)S(1)}, bf16[8,128,384]{1,2,0:T(8,128)(2,1)}, u32[]{:S(2)}) copy-start(bf16[8,128,384]{1,2,0:T(8,128)(2,1)} %get-tuple-element.241) | copy-start | bytes 2359300
  388.8 116.0 %reduce-scatter.6.cloned.1.call-start = ((), (), s32[]{:S(2)}) async-start(), calls=%async_computation.5 | async-start | bytes 2457600 | tf_op jit(solution)/shard_map/reduce_scatter | solution.py:24
  471.4 72.4 %reduce-scatter.8.cloned.1.call-start = ((), (), s32[]{:S(2)}) async-start(), calls=%async_computation.6 | async-start | bytes 737280 | tf_op jit(solution)/shard_map/reduce_scatter | solution.py:24
  471.7 33.6 %collective-permute-start = (bf16[512,384]{1,0:T(8,128)(2,1)S(1)}, bf16[512,384]{1,0:T(8,128)(2,1)}, u32[]{:S(2)}, u32[]{:S(2)}) collective-permute-start(bf16[512,384]{1,0:T(8,128)(2,1)S(1)} %bitcast.201), channel_id=1, source_target_pairs={{0,128},{8,136},{16,144},{24,152},{32,160},{40,168},{48,176},{56,1... | collective-permute-start | bytes 1179656 | tf_op jit(solution)/shard_map/ppermute | solution.py:15
  477.2 1.9 copy-start.2
  479.0 26.3 %collective-permute-start.1 = (bf16[512,384]{1,0:T(8,128)(2,1)S(1)}, bf16[512,384]{1,0:T(8,128)(2,1)}, u32[]{:S(2)}, u32[]{:S(2)}) collective-permute-start(bf16[512,384]{1,0:T(8,128)(2,1)S(1)} %slice.154), channel_id=1, source_target_pairs={{0,128},{8,136},{16,144},{24,152},{32,160},{40,168},{48,176},{56,1... | collective-permute-start | bytes 1179656 | tf_op jit(solution)/shard_map/ppermute | solution.py:15
  479.1 5.5 %copy-start.10 = (s32[32]{0:T(128)S(1)}, s32[32]{0:T(128)}, u32[]{:S(2)}) copy-start(s32[32]{0:T(128)} %param.39) | copy-start | bytes 388
  479.3 37.8 %collective-permute-start.2 = (bf16[512,384]{1,0:T(8,128)(2,1)S(1)}, bf16[512,384]{1,0:T(8,128)(2,1)}, u32[]{:S(2)}, u32[]{:S(2)}) collective-permute-start(bf16[512,384]{1,0:T(8,128)(2,1)S(1)} %slice.156), channel_id=1, source_target_pairs={{0,128},{8,136},{16,144},{24,152},{32,160},{40,168},{48,176},{56,1... | collective-permute-start | bytes 1179656 | tf_op jit(solution)/shard_map/ppermute | solution.py:15
  519.5 24.2 %copy-start.1 = (s32[32,8]{0,1:T(8,128)S(1)}, s32[32,8]{0,1:T(8,128)}, u32[]{:S(2)}) copy-start(s32[32,8]{0,1:T(8,128)} %param.38) | copy-start | bytes 3076
Sparse Core Ops, SparseCore 0:
  9.8 115.2 all-gather.1
  388.9 82.3 reduce-scatter.3
  473.9 30.9 reduce-scatter.5
  507.8 35.8 reduce-scatter.7
where the time goes:
time: 553 us; the launch traced here: 550 us
  waiting for transfers between devices  253 us (46%)
  local copies, waits for them, and re-layouts  113 us (20%)
  loops' own time  71.5 us (13%)
  matrix products  44.1 us (8%)
  other arithmetic  42.3 us (8%)
  between operations  14.6 us (3%)
  starting transfers between devices  11.2 us (2%)
    reduce_scatter x3, waiting for transfers between devices, reduced_to_own(): tiles = lax.psum_scatter(tiles, axes[k], scatter_dimension=0, tiled=True)  124 us
    all_gather x1, waiting for transfers between devices, shards(): full_gradient = lax.all_gather(out_gradient, 'tensor', axis=0, tiled=True)  117 us
    another operation x1, loops' own time, attend(): lax.scan(visit, start_totals, jnp.arange(total_blocks, dtype=jnp.int32))  68.9 us
    dynamic_slice x16, local copies, waits for them, and re-layouts, visit(): lax.dynamic_slice_in_dim(value_total, start * BLOCK, window * BLOCK, 0)  13.9 us
    dynamic_update_slice x24, local copies, waits for them, and re-layouts, attend(): lax.scan(visit, start_totals, jnp.arange(total_blocks, dtype=jnp.int32))  11.8 us
    dot_general x1, matrix products, shards(): lax.dot_general(full_gradient, head_output, (((0,), (0,)), ((), ())), pre...  11.7 us
    ppermute x3, waiting for transfers between devices, swapped(): lax.ppermute(x, axis, [(i, i ^ 1 << distance) for i in range(lax.axis_siz...  11.7 us
    ppermute x3, starting transfers between devices, swapped(): lax.ppermute(x, axis, [(i, i ^ 1 << distance) for i in range(lax.axis_siz...  11.1 us
  transfers between devices with their start and end apart: 7, of which 5 were waited for; matrix products, arithmetic and copies ran while one was open for 1% of the time, Pallas kernels for 0%

commit v1 on v0

--- a/solution.py
+++ b/solution.py
@@ -172,7 +172,9 @@
 
 
 def shards(queries, keys, values, out_gradient, out_weight, segments, counts):
-    full_gradient = lax.all_gather(out_gradient, "tensor", axis=0, tiled=True)
+    full_gradient = jnp.concatenate(
+        lax.all_to_all(jnp.stack([out_gradient] * lax.axis_size("tensor")), "tensor", 0, 0), axis=0
+    )
     head_gradient = lax.dot_general(
         full_gradient, out_weight, (((1,), (1,)), ((), ())), preferred_element_type=jnp.float32
     ).astype(jnp.bfloat16)

time: 553 us -> 840 us (1.52)
  waiting for transfers between devices: 253 us -> 379 us
  local copies, waits for them, and re-layouts: 113 us -> 180 us
  matrix products: 44.1 us -> 108 us
  other arithmetic: 42.3 us -> 61.3 us
    all_to_all x0 -> x1, waiting for transfers between devices: none -> 228 us  [shards(): lax.all_to_all(jnp.stack([out_gradient] * lax.axis_size('tensor')), 'tens...]
    all_gather x1 -> x0, waiting for transfers between devices: 117 us -> none  [shards(): full_gradient = lax.all_gather(out_gradient, 'tensor', axis=0, tiled=True)]
    while x160 -> x384, local copies, waits for them, and re-layouts: 8.24 us -> 63.5 us
    dot_general x20, matrix products: 3.8 us -> 27.2 us  [visit(): jnp.einsum('hqk,khd->qhd', weight_tile, value_tile, preferred_element_typ...]
    dot_general x20, matrix products: 4.4 us -> 22.3 us  [near(): jnp.einsum('qhd,khd->hqk', grad_block, value_tile, preferred_element_type...]
    reduce_scatter x3, waiting for transfers between devices: 124 us -> 139 us  [reduced_to_own(): tiles = lax.psum_scatter(tiles, axes[k], scatter_dimension=0, tiled=True)]
    another operation x50 -> x51, local copies, waits for them, and re-layouts: 3.23 us -> 14.2 us
    dot_general x20, matrix products: 3.91 us -> 14.6 us  [near_back(): jnp.einsum('hqk,khd->qhd', slope_tile, key_tile, preferred_element_type=j...]
where the time goes in v1:
time: 840 us; the launch traced here: 834 us
  waiting for transfers between devices  379 us (45%)
  local copies, waits for them, and re-layouts  180 us (21%)
  matrix products  108 us (13%)
  loops' own time  71.6 us (9%)
  other arithmetic  61.3 us (7%)
  starting transfers between devices  19.4 us (2%)
  between operations  14.5 us (2%)
    all_to_all x1, waiting for transfers between devices, shards(): lax.all_to_all(jnp.stack([out_gradient] * lax.axis_size('tensor')), 'tens...  228 us
    reduce_scatter x3, waiting for transfers between devices, reduced_to_own(): tiles = lax.psum_scatter(tiles, axes[k], scatter_dimension=0, tiled=True)  139 us
    another operation x1, loops' own time, attend(): lax.scan(visit, start_totals, jnp.arange(total_blocks, dtype=jnp.int32))  69.4 us
    while x384, local copies, waits for them, and re-layouts  63.5 us
    dot_general x20, matrix products, visit(): jnp.einsum('hqk,khd->qhd', weight_tile, value_tile, preferred_element_typ...  27.2 us
    dot_general x20, matrix products, near(): jnp.einsum('qhd,khd->hqk', grad_block, value_tile, preferred_element_type...  22.3 us
  transfers between devices with their start and end apart: 7, of which 5 were waited for; matrix products, arithmetic and copies ran while one was open for 1% of the time, Pallas kernels for 0%

profile of v1, /device:TPU:1, one launch (start us, length us, event | category | flops | bytes accessed | tf_op | source)
XLA Modules:
  0.0 834.0 jit_solution(5396223296286677592)
XLA Ops:
  7.2 6.6 stack.2
  13.8 8.2 all-to-all-start
  22.2 227.8 %all-to-all-done = bf16[8,128,5120]{2,1,0:T(8,128)(2,1)} async-done(((bf16[8,128,5120]{2,1,0:T(8,128)(2,1)}), bf16[8,128,5120]{2,1,0:T(8,128)(2,1)}, u32[]{:S(2)}, u32[]{:S(2)}) %all-to-all-start) | async-done | bytes 10485792 | tf_op jit(solution)/shard_map/all_to_all | solution.py:176
  250.0 10.2 %convolution_convert_fusion = bf16[1024,384]{1,0:T(8,128)(2,1)} fusion(bf16[1024,5120]{1,0:T(8,128)(2,1)} %bitcast.43, bf16[384,5120]{1,0:T(8,128)(2,1)} %param.37), kind=kOutput, calls=%fused_computation.58 | convolution fusion | flops 4026925056 | bytes 15204352 | tf_op jit(solution)/shard_map/dot_general | solution.py:178
  261.6 368.1 %while.16 = (s32[]{:T(128)}, f32[1024,384]{1,0:T(8,128)}, f32[1024,384]{1,0:T(8,128)S(1)}, bf16[8,128,384]{1,2,0:T(8,128)(2,1)}, bf16[8,128,384]{1,2,0:T(8,128)(...) while((s32[]{:T(128)}, f32[1024,384]{1,0:T(8,128)}, ...), condition=%wide.region_32.33_spmd, body=%wide.region_0.32_spmd.sunk | while | flops 308919232 | bytes 64811208 | solution.py:166
  278.3 2.3 conditional.27
  287.4 1.7 multiply_reduce_fusion.2
  289.1 1.5 fusion.84
  319.1 2.3 conditional.27
  328.2 1.7 multiply_reduce_fusion.2
  329.9 1.5 fusion.84
  360.0 2.3 conditional.27
  369.1 1.7 multiply_reduce_fusion.2
  370.8 1.5 fusion.84
  400.8 2.3 conditional.27
  409.9 1.7 multiply_reduce_fusion.2
  411.6 1.5 fusion.84
  413.1 1.4 conditional.35
  444.3 2.3 conditional.27
  449.5 2.3 conditional.26
  455.3 1.8 conditional.29
  455.3 1.8 convolution_bitcast_fusion.2
  457.0 1.8 conditional.28
  457.0 1.8 convolution_bitcast_fusion.3
  458.8 1.7 multiply_reduce_fusion.2
  460.5 1.5 fusion.84
  462.0 1.4 conditional.35
  495.5 2.3 conditional.27
  500.6 2.3 conditional.26
  506.4 1.8 conditional.29
  506.4 1.8 convolution_bitcast_fusion.2
  508.2 1.8 conditional.28
  508.2 1.8 convolution_bitcast_fusion.3
  510.0 1.7 multiply_reduce_fusion.2
  511.7 1.5 fusion.84
  513.2 1.4 conditional.35
  514.6 1.4 conditional.34
  546.6 2.3 conditional.27
  551.8 2.3 conditional.26
  557.6 1.8 conditional.29
  557.6 1.8 convolution_bitcast_fusion.2
  559.3 1.8 conditional.28
  559.3 1.8 convolution_bitcast_fusion.3
  561.1 1.7 multiply_reduce_fusion.2
  562.8 1.5 fusion.84
  597.8 2.3 conditional.27
  602.9 2.3 conditional.26
  608.7 1.8 conditional.29
  608.7 1.8 convolution_bitcast_fusion.2
  610.5 1.8 conditional.28
  610.5 1.8 convolution_bitcast_fusion.3
  612.3 1.7 multiply_reduce_fusion.2
  614.0 1.5 fusion.84
  629.6 9.0 %fusion.17 = f32[5120,384]{0,1:T(8,128)} fusion(bf16[8,128,384]{1,2,0:T(8,128)(2,1)} %get-tuple-element.244, bf16[8,128,5120]{2,1,0:T(8,128)(2,1)} %all-to-all-done), kind=kOutput, calls=%fused_computation.56 | convolution fusion | flops 4028497920 | bytes 19136512 | tf_op jit(solution)/shard_map/dot_general | solution.py:207
  638.6 9.1 %copy.85 = f32[5120,384]{1,0:T(8,128)} copy(f32[5120,384]{0,1:T(8,128)} %fusion.17) | data formatting | bytes 15728640 | tf_op jit(solution)/shard_map/div | solution.py:207
  647.7 7.1 copy.86
  654.9 99.2 %reduce-scatter.4.cloned.1.call-done = f32[8,160,384]{2,1,0:T(8,128)} async-done(((f32[32,160,384]{2,1,0:T(8,128)}), f32[8,160,384]{2,1,0:T(8,128)}) %reduce-scatter.4.cloned.1.call-update) | async-done | bytes 1966096 | tf_op jit(solution)/shard_map/reduce_scatter | solution.py:24
  755.3 5.4 collective-permute-start
  760.8 1.6 multiply_convert_fusion.1
  763.2 5.5 collective-permute-start.2
  769.9 17.6 %reduce-scatter.6.cloned.1.call-done = f32[2,160,384]{2,1,0:T(8,128)} async-done(((f32[8,160,384]{2,1,0:T(8,128)}), f32[2,160,384]{2,1,0:T(8,128)}) %reduce-scatter.6.cloned.1.call-update) | async-done | bytes 491536 | tf_op jit(solution)/shard_map/reduce_scatter | solution.py:24
  788.0 12.9 %collective-permute-done.2 = bf16[512,384]{1,0:T(8,128)(2,1)} collective-permute-done((bf16[512,384]{1,0:T(8,128)(2,1)S(1)}, bf16[512,384]{1,0:T(8,128)(2,1)}, u32[]{:S(2)}, u32[]{:S(2)}) %collective-permute-start.2) | collective-permute-done | bytes 393248 | tf_op jit(solution)/shard_map/ppermute | solution.py:15
  800.9 1.7 fusion.20
  805.5 21.9 %reduce-scatter.8.cloned.1.call-done = f32[1,160,384]{2,1,0:T(8,128)} async-done(((f32[2,160,384]{2,1,0:T(8,128)}), f32[1,160,384]{2,1,0:T(8,128)}) %reduce-scatter.8.cloned.1.call-update) | async-done | bytes 245776 | tf_op jit(solution)/shard_map/reduce_scatter | solution.py:24
  (908 shorter events, 317.1 us)
Async XLA Ops:
  7.2 14.9 %copy-start = (s32[32,8]{0,1:T(8,128)S(1)}, s32[32,8]{0,1:T(8,128)}, u32[]{:S(2)}) copy-start(s32[32,8]{0,1:T(8,128)} %param.38) | copy-start | bytes 3076
  13.8 236.2 %all-to-all-start = ((bf16[8,128,5120]{2,1,0:T(8,128)(2,1)}), bf16[8,128,5120]{2,1,0:T(8,128)(2,1)}, u32[]{:S(2)}, u32[]{:S(2)}) async-start(bf16[8,128,5120]{2,1,0:T(8,128)(2,1)} %stack.2), calls=%async_computation | async-start | bytes 20971520 | tf_op jit(solution)/shard_map/all_to_all | solution.py:176
  22.0 732.0 %reduce-scatter.4.cloned.1.call-start = ((), (), s32[]{:S(2)}) async-start(), calls=%async_computation.4 | async-start | bytes 9830400 | tf_op jit(solution)/shard_map/reduce_scatter | solution.py:24
  261.6 33.6 %copy-start.2 = (f32[1024,384]{1,0:T(8,128)}, f32[1024,384]{1,0:T(8,128)S(1)}, u32[]{:S(2)}) copy-start(f32[1024,384]{1,0:T(8,128)S(1)} %get-tuple-element.600) | copy-start | bytes 4718596 | tf_op jit(solution)/shard_map/while
  272.9 2.3 copy-start.17
  275.3 2.9 copy-start.18
  280.5 3.1 copy-start.19
  298.9 1.5 copy-start.16
  300.8 1.7 copy-start.3
  302.5 33.6 %copy-start.2 = (f32[1024,384]{1,0:T(8,128)}, f32[1024,384]{1,0:T(8,128)S(1)}, u32[]{:S(2)}) copy-start(f32[1024,384]{1,0:T(8,128)S(1)} %get-tuple-element.600) | copy-start | bytes 4718596 | tf_op jit(solution)/shard_map/while
  313.8 2.3 copy-start.17
  316.2 2.9 copy-start.18
  321.4 3.1 copy-start.19
  339.8 1.5 copy-start.16
  341.6 1.7 copy-start.3
  343.3 33.6 %copy-start.2 = (f32[1024,384]{1,0:T(8,128)}, f32[1024,384]{1,0:T(8,128)S(1)}, u32[]{:S(2)}) copy-start(f32[1024,384]{1,0:T(8,128)S(1)} %get-tuple-element.600) | copy-start | bytes 4718596 | tf_op jit(solution)/shard_map/while
  354.7 2.3 copy-start.17
  357.0 2.9 copy-start.18
  362.2 3.1 copy-start.19
  380.6 1.5 copy-start.16
  382.5 1.7 copy-start.3
  384.2 33.6 %copy-start.2 = (f32[1024,384]{1,0:T(8,128)}, f32[1024,384]{1,0:T(8,128)S(1)}, u32[]{:S(2)}) copy-start(f32[1024,384]{1,0:T(8,128)S(1)} %get-tuple-element.600) | copy-start | bytes 4718596 | tf_op jit(solution)/shard_map/while
  395.5 2.3 copy-start.17
  397.9 2.9 copy-start.18
  403.1 3.1 copy-start.19
  421.5 1.5 copy-start.16
  423.3 1.7 copy-start.3
  425.0 43.9 %copy-start.2 = (f32[1024,384]{1,0:T(8,128)}, f32[1024,384]{1,0:T(8,128)S(1)}, u32[]{:S(2)}) copy-start(f32[1024,384]{1,0:T(8,128)S(1)} %get-tuple-element.600) | copy-start | bytes 4718596 | tf_op jit(solution)/shard_map/while
  437.7 2.3 copy-start.17
  441.4 2.9 copy-start.18
  446.6 5.3 copy-start.19
  463.5 1.5 copy-start.4
  463.5 1.5 copy-start.6
  472.6 1.5 copy-start.16
  474.5 1.7 copy-start.3
  476.2 43.9 %copy-start.2 = (f32[1024,384]{1,0:T(8,128)}, f32[1024,384]{1,0:T(8,128)S(1)}, u32[]{:S(2)}) copy-start(f32[1024,384]{1,0:T(8,128)S(1)} %get-tuple-element.600) | copy-start | bytes 4718596 | tf_op jit(solution)/shard_map/while
  488.8 2.3 copy-start.17
  492.5 2.9 copy-start.18
  497.7 5.3 copy-start.19
  514.6 1.5 copy-start.4
  514.6 1.5 copy-start.6
  525.6 1.7 copy-start.3
  527.3 43.9 %copy-start.2 = (f32[1024,384]{1,0:T(8,128)}, f32[1024,384]{1,0:T(8,128)S(1)}, u32[]{:S(2)}) copy-start(f32[1024,384]{1,0:T(8,128)S(1)} %get-tuple-element.600) | copy-start | bytes 4718596 | tf_op jit(solution)/shard_map/while
  540.0 2.3 copy-start.17
  543.7 2.9 copy-start.18
  548.9 5.3 copy-start.19
  565.8 1.5 copy-start.4
  565.8 1.5 copy-start.6
  576.8 1.7 copy-start.3
  578.5 43.9 %copy-start.2 = (f32[1024,384]{1,0:T(8,128)}, f32[1024,384]{1,0:T(8,128)S(1)}, u32[]{:S(2)}) copy-start(f32[1024,384]{1,0:T(8,128)S(1)} %get-tuple-element.600) | copy-start | bytes 4718596 | tf_op jit(solution)/shard_map/while
  591.1 2.3 copy-start.17
  594.8 2.9 copy-start.18
  600.0 5.3 copy-start.19
  616.9 1.5 copy-start.4
  616.9 1.5 copy-start.6
  627.9 1.7 copy-start.3
  654.8 99.5 %copy-start.22 = (bf16[8,128,384]{1,2,0:T(8,128)(2,1)S(1)}, bf16[8,128,384]{1,2,0:T(8,128)(2,1)}, u32[]{:S(2)}) copy-start(bf16[8,128,384]{1,2,0:T(8,128)(2,1)} %get-tuple-element.241) | copy-start | bytes 2359300
  654.8 132.8 %reduce-scatter.6.cloned.1.call-start = ((), (), s32[]{:S(2)}) async-start(), calls=%async_computation.5 | async-start | bytes 2457600 | tf_op jit(solution)/shard_map/reduce_scatter | solution.py:24
  754.1 73.4 %reduce-scatter.8.cloned.1.call-start = ((), (), s32[]{:S(2)}) async-start(), calls=%async_computation.6 | async-start | bytes 737280 | tf_op jit(solution)/shard_map/reduce_scatter | solution.py:24
  755.3 32.7 %collective-permute-start = (bf16[512,384]{1,0:T(8,128)(2,1)}, bf16[512,384]{1,0:T(8,128)(2,1)}, u32[]{:S(2)}, u32[]{:S(2)}) collective-permute-start(bf16[512,384]{1,0:T(8,128)(2,1)} %bitcast.47), channel_id=1, source_target_pairs={{0,128},{8,136},{16,144},{24,152},{32,160},{40,168},{48,176},{56,1... | collective-permute-start | bytes 1179656 | tf_op jit(solution)/shard_map/ppermute | solution.py:15
  763.1 24.9 %collective-permute-start.1 = (bf16[512,384]{1,0:T(8,128)(2,1)}, bf16[512,384]{1,0:T(8,128)(2,1)}, u32[]{:S(2)}, u32[]{:S(2)}) collective-permute-start(bf16[512,384]{1,0:T(8,128)(2,1)} %slice.154), channel_id=1, source_target_pairs={{0,128},{8,136},{16,144},{24,152},{32,160},{40,168},{48,176},{56,1... | collective-permute-start | bytes 1179656 | tf_op jit(solution)/shard_map/ppermute | solution.py:15
  763.1 5.6 copy-start.23
  763.2 37.7 %collective-permute-start.2 = (bf16[512,384]{1,0:T(8,128)(2,1)S(1)}, bf16[512,384]{1,0:T(8,128)(2,1)}, u32[]{:S(2)}, u32[]{:S(2)}) collective-permute-start(bf16[512,384]{1,0:T(8,128)(2,1)S(1)} %slice.156), channel_id=1, source_target_pairs={{0,128},{8,136},{16,144},{24,152},{32,160},{40,168},{48,176},{56,1... | collective-permute-start | bytes 1179656 | tf_op jit(solution)/shard_map/ppermute | solution.py:15
  803.6 23.8 %copy-start.1 = (s32[32,8]{0,1:T(8,128)S(1)}, s32[32,8]{0,1:T(8,128)}, u32[]{:S(2)}) copy-start(s32[32,8]{0,1:T(8,128)} %param.38) | copy-start | bytes 3076
  (107 other events, 101.7 us)
Sparse Core Ops, SparseCore 0:
  654.9 99.1 reduce-scatter.3
  756.6 30.8 reduce-scatter.5
  790.7 36.7 reduce-scatter.7
